TPU v7x, 32 devices: a whole 2x2x4 slice. The times are simulated.
32 devices in a mesh: row: 4 (over y, x), col: 8 (over z, core).
Axes of the slice: x: 2, y: 2, z: 4, core: 2. Of those that a mesh axis runs over, the one named last changes fastest.
Arguments:
- tile_left: bfloat16 [4, 16, 2048, 64], P('row', 'col'), may hold values from -6 to 6
- tile_right: bfloat16 [4, 16, 2048, 64], P('row', 'col'), may hold values from -0.75 to 0.75
- panel_rows: bfloat16 [4, 2048, 128], P('row', 'col'), may hold values from -0.71875 to 0.71875
- panel_cols: bfloat16 [16, 2048, 128], P('col', 'row'), may hold values from -0.71875 to 0.71875
- vectors: bfloat16 [16, 2048, 32], P('col', 'row'), may hold values from -0.033203125 to 0.033203125
- omega: bfloat16 [2048, 64], replicated, may hold values from -0.125 to 0.125
- psi: bfloat16 [2048, 64], replicated, may hold values from -0.125 to 0.125
Outputs:
- sketch_left: bfloat16 [4, 16, 2048, 64], P('row', 'col')
- sketch_right: bfloat16 [4, 16, 2048, 64], P('row', 'col')
- product: float32 [4, 2048, 32], P('row', 'col')
All inputs are finite; a program needn't handle non-finite values.
Results may differ from a plain program's by a relative error of at most 0.0049.
Values may be sent and summed in bfloat16 or wider, within the bound.
No kernel may reach another device: no remote copies, remote signals or barrier semaphores. Data moves between devices by JAX's collectives and lax.ppermute only.
A program may use at most 64 MiB of HBM per device.

v0:
```python
import functools

import jax
import jax.numpy as jnp
from jax import lax
from jax.experimental import pallas as pl
from jax.experimental.pallas import tpu as pltpu
from jax.sharding import PartitionSpec as P


F32 = jnp.float32
BF16 = jnp.bfloat16
HI = lax.Precision.HIGHEST
LANES = 128


def nn(a, b, precision=None):
    return lax.dot_general(
        a, b, (((1,), (0,)), ((), ())), precision=precision, preferred_element_type=F32
    )


def nt(a, b, precision=None):
    return lax.dot_general(
        a, b, (((1,), (1,)), ((), ())), precision=precision, preferred_element_type=F32
    )


def tn(a, b):
    return lax.dot_general(a, b, (((0,), (0,)), ((), ())), preferred_element_type=F32)


def call(kernel, out_shape, *args, hbm=(), raw=(), scratch=()):
    vm, anywhere = pl.BlockSpec(memory_space=pltpu.VMEM), pl.BlockSpec(memory_space=pl.ANY)
    spaces = [pltpu.HBM if k in hbm or k in raw else pltpu.VMEM for k in range(len(args))]
    args = [pltpu.with_memory_space_constraint(x, space) for x, space in zip(args, spaces)]
    return pl.pallas_call(
        kernel,
        out_shape=out_shape,
        in_specs=[anywhere if k in raw else vm for k in range(len(args))],
        out_specs=jax.tree.map(lambda _: vm, out_shape),
        scratch_shapes=list(scratch),
        compiler_params=pltpu.CompilerParams(vmem_limit_bytes=16 << 20),
    )(*args)


def add_all(xs):
    return functools.reduce(lambda a, b: a + b, xs)


def at_block(index, size):
    return pl.ds(pl.multiple_of(index * size, size), size)


def pack_kernel(tiles, rank, cols_ref, vec_ref, u_ref, v_ref):
    chunk, nvec = cols_ref.shape[1], vec_ref.shape[1]
    u = jnp.concatenate([cols_ref[t, :, :rank] for t in range(tiles)], axis=1)
    u_ref[...] = u
    v_ref[:chunk] = jnp.concatenate([cols_ref[t, :, rank:] for t in range(tiles)], axis=1)
    part = nn(vec_ref[...].reshape(tiles * nvec, chunk), u)
    base = chunk
    for b in range(chunk // LANES):
        for t in range(tiles):
            v_ref[base : base + nvec] = vec_ref[t, :, b * LANES : (b + 1) * LANES]
            base += nvec
    part = [part[t * nvec : (t + 1) * nvec, t * rank : (t + 1) * rank] for t in range(tiles)]
    v_ref[base:] = jnp.concatenate(part, axis=1).astype(BF16)


def load_kernel(tiles, *refs):
    sources, targets, (coef_a, coef_c), sems = refs[:4], refs[4:8], refs[8:10], refs[10]
    copies = [
        pltpu.make_async_copy(s, t, sems.at[k]) for k, (s, t) in enumerate(zip(sources, targets))
    ]
    for copy in copies:
        copy.start()
    for copy in copies:
        copy.wait()
    left, right, omega, psi = targets
    for t in range(tiles):
        coef_a[t] = nt(omega[...], right[t]).astype(BF16)
        coef_c[t] = nt(psi[...], left[t]).astype(BF16)


def pair_kernel(own, other, both):
    size = own.shape[0]
    core = lax.axis_index("col") & 1
    both[at_block(core, size), :] = own[...]
    both[at_block(1 - core, size), :] = other[...]


def gram_kernel(tiles, rank, nvec, rparts, cparts, split, ways, *refs):
    left, right = refs[:2]
    rows, refs = refs[2 : 3 + 2 * len(ways)], refs[3 + 2 * len(ways) :]
    vs, gram_out, rows_full = refs[:rparts], refs[rparts], refs[rparts + 1]
    rest, vec_full = refs[rparts + 2 : -1], refs[-1]
    row, col = lax.axis_index("row"), lax.axis_index("col")
    size = rows_full.shape[0] // cparts
    core, chip = col & 1, col >> 1
    rows_full[at_block(chip, 2 * size), :] = rows[0][...]
    for (one, two), mine, other in zip(ways, rows[1::2], rows[2::2]):
        if one == two:
            at = 2 * (chip ^ one)
            rows_full[at_block(at + core, size), :] = mine[...]
            rows_full[at_block(at + 1 - core, size), :] = other[...]
        else:
            rows_full[at_block(chip ^ (one + core * (two - one)), 2 * size), :] = mine[...]
            rows_full[at_block(chip ^ (two + core * (one - two)), 2 * size), :] = other[...]
    chunk = left.shape[2] // rparts
    blocks = chunk // LANES
    wide = tiles * nvec
    for k in range(rparts):
        for b in range(blocks):
            at = chunk + b * wide
            vec_full[:, at_block((row ^ k) * blocks + b, LANES)] = vs[k][at : at + wide]
    gram = add_all(
        [tn(rows_full[at_block(row ^ k, chunk), :], vs[k][:chunk]) for k in range(rparts)]
    )[rank:, :]
    gram_out[...] = gram
    coef_p = [
        nt(vec_full[t * nvec : (t + 1) * nvec], right[t]).astype(BF16) for t in range(tiles)
    ]
    total = add_all([nn(coef_p[t], left[t]) for t in range(tiles)])
    proj = add_all([v[chunk + blocks * wide :].astype(F32) for v in vs])
    coef_q = nt(proj, gram, HI).astype(BF16)
    padded = jnp.concatenate([coef_q, jnp.zeros_like(coef_q)], axis=1)
    total = total - nt(padded, rows_full[...])
    if split:
        keep, send, full = rest
        full[...] = total
        for m in range(cparts // 2):
            keep[m] = full[:, at_block(col ^ (2 * m), size)]
            send[m] = full[:, at_block(col ^ (2 * m + 1), size)].astype(BF16)
    else:
        rest[0][...] = total


def final_kernel(tiles, rank, parts, *refs):
    left, right, omega, psi, coef_a, coef_c, gram, rows_full = refs[:8]
    us = refs[8 : 8 + parts]
    out_first, out_second = refs[8 + parts :]
    row = lax.axis_index("row")
    chunk = us[0].shape[0]
    width = omega.shape[0]
    lane = lax.broadcasted_iota(jnp.int32, (width, tiles * rank), 1)
    gram_all = gram[...]
    row_sketch = nn(psi[...], rows_full[...])[:, :rank]
    coef_d = nn(row_sketch, gram_all, HI)
    sketch = add_all(
        [nn(omega[:, at_block(row ^ k, chunk)], us[k][...]) for k in range(parts)]
    )
    lows, ds = [], []
    for t in range(tiles):
        mine = (lane >= t * rank) & (lane < (t + 1) * rank)
        coef_b = nt(jnp.where(mine, sketch, 0.0), gram_all, HI).astype(BF16)
        lows.append(jnp.concatenate([coef_b, jnp.zeros_like(coef_b)], axis=1))
        ds.append(jnp.where(mine, coef_d, 0.0).astype(BF16))
    low = nt(jnp.concatenate(lows, axis=0), rows_full[...])
    for t in range(tiles):
        first = nn(coef_a[t], left[t])
        out_first[t] = (first - low[t * width : (t + 1) * width]).astype(BF16)
    coefs = jnp.concatenate(ds, axis=0)
    for k in range(parts):
        at = at_block(row ^ k, chunk)
        low = nt(coefs, us[k][...])
        for t in range(tiles):
            second = nn(coef_c[t], right[t, :, at])
            out_second[t, :, at] = (second - low[t * width : (t + 1) * width]).astype(BF16)


def routes(n_col):
    far = list(range(n_col // 2 - 1, 0, -1))
    return [(far[0], far[0])] * (len(far) % 2) + list(
        zip(far[len(far) % 2 :: 2], far[len(far) % 2 + 1 :: 2])
    )


def local(n_row, n_col, tile_left, tile_right, panel_rows, panel_cols, vectors, omega, psi):
    tiles, order, rank = tile_left.shape[1:]
    nvec = vectors.shape[2]
    chunk = panel_cols.shape[1]
    size = panel_rows.shape[1]
    wide = omega.shape[1]
    half = n_col // 2

    def swap(axis, count, value, m):
        return lax.ppermute(value, axis, [(i, i ^ m) for i in range(count)])

    def row_swap(value, m):
        return swap("row", n_row, value, m)

    def col_swap(value, m):
        return swap("col", n_col, value, m)

    left = jnp.swapaxes(tile_left[0], 1, 2)
    right = jnp.swapaxes(tile_right[0], 1, 2)
    vec = jnp.swapaxes(vectors, 1, 2)
    omega_t, psi_t = omega.T, psi.T
    rows = panel_rows[0]
    vmem = pltpu.VMEM

    u, v = call(
        functools.partial(pack_kernel, tiles, rank),
        (
            vmem((chunk, tiles * rank), BF16),
            vmem((chunk + tiles * nvec * chunk // LANES + nvec, tiles * rank), BF16),
        ),
        panel_cols,
        vec,
        hbm=(0, 1),
    )
    sources = (left, right, omega_t, psi_t)
    left, right, omega_t, psi_t, coef_a, coef_c = call(
        functools.partial(load_kernel, tiles),
        tuple(vmem(x.shape, BF16) for x in sources)
        + (vmem((tiles, wide, rank), BF16), vmem((tiles, wide, rank), BF16)),
        *sources,
        raw=(0, 1, 2, 3),
        scratch=[pltpu.SemaphoreType.DMA((4,))],
    )
    vs = [v] + [row_swap(v, k) for k in range(1, n_row)]
    us = [u] + [row_swap(u, k) for k in range(1, n_row)]
    both = call(pair_kernel, vmem((2 * size, 2 * rank), BF16), rows, col_swap(rows, 1))
    ways = routes(n_col)
    row_parts = [both]
    for one, two in ways:
        perm = [(i, i ^ (2 * (two if i % 2 else one))) for i in range(n_col)]
        got = lax.ppermute(rows if one == two else both, "col", perm)
        row_parts += [got, col_swap(got, 1)]

    split = size % LANES == 0
    outs = (
        vmem((rank, tiles * rank), F32),
        vmem((order, 2 * rank), BF16),
    )
    if split:
        outs += (vmem((half, nvec, size), F32), vmem((half, nvec, size), BF16))
    else:
        outs += (vmem((nvec, order), F32),)
    scratch = [pltpu.VMEM((tiles * nvec, order), BF16)]
    gram, rows_full, *rest = call(
        functools.partial(gram_kernel, tiles, rank, nvec, n_row, n_col, split, ways),
        outs,
        left,
        right,
        *row_parts,
        *vs,
        scratch=([pltpu.VMEM((nvec, order), F32)] if split else []) + scratch,
    )
    if split:
        keep, send = rest
    else:
        col = lax.axis_index("col")
        blocks = rest[0].reshape(nvec, n_col, size).swapaxes(0, 1)
        where = col ^ (2 * jnp.arange(half))
        keep = blocks[where]
        send = blocks[where ^ 1].astype(BF16)
    got = col_swap(send, 1)
    mine = keep[0] + got[0].astype(F32)
    arrived = [col_swap((keep[m] + got[m].astype(F32)).astype(BF16), 2 * m) for m in range(1, half)]
    out_first, out_second = call(
        functools.partial(final_kernel, tiles, rank, n_row),
        (
            jax.ShapeDtypeStruct((tiles, wide, order), BF16),
            jax.ShapeDtypeStruct((tiles, wide, order), BF16),
        ),
        left,
        right,
        omega_t,
        psi_t,
        coef_a,
        coef_c,
        gram,
        rows_full,
        *us,
    )
    for x in arrived:
        mine = mine + x.astype(F32)
    return (
        jnp.swapaxes(out_first, 1, 2)[None],
        jnp.swapaxes(out_second, 1, 2)[None],
        mine.T[None],
    )


def solution(mesh):
    in_specs = (
        P("row", "col", None, None),
        P("row", "col", None, None),
        P("row", "col", None),
        P("col", "row", None),
        P("col", "row", None),
        P(),
        P(),
    )
    out_specs = (P("row", "col", None, None), P("row", "col", None, None), P("row", "col", None))
    n_row, n_col = mesh.shape["row"], mesh.shape["col"]

    def body(*args):
        return local(n_row, n_col, *args)

    return jax.shard_map(body, mesh=mesh, in_specs=in_specs, out_specs=out_specs, check_vma=False)
```

profile of v0, /device:TPU:0, one launch (start us, length us, event | category | flops | bytes accessed | tf_op | source)
XLA Modules:
  0.0 35.0 jit_solution(2548010700106842329)
XLA Ops:
  0.6 0.6 %collective-permute-start = (bf16[256,128]{1,0:T(8,128)(2,1)}, bf16[256,128]{1,0:T(8,128)(2,1)S(1)}, u32[]{:S(2)}, u32[]{:S(2)}) collective-permute-start(bf16[256,128]{1,0:T(8,128)(2,1)} %bitcast.34), channel_id=1, source_target_pairs={{0,1},{1,0},{2,3},{3,2},{4,5},{5,4},{6,7},{7,6},{8,9},{9,8},{10,11... | collective-permute-start | bytes 196616 | tf_op jit(solution)/shard_map/ppermute | solution.py:187
  1.2 1.1 %collective-permute-done.other = bf16[256,128]{1,0:T(8,128)(2,1)S(1)} collective-permute-done((bf16[256,128]{1,0:T(8,128)(2,1)}, bf16[256,128]{1,0:T(8,128)(2,1)S(1)}, u32[]{:S(2)}, u32[]{:S(2)}) %collective-permute-start) | collective-permute-done | bytes 65568 | tf_op jit(solution)/shard_map/ppermute | solution.py:187
  2.3 0.0 copy-start
  2.3 0.8 %copy-done = bf16[1,256,128]{2,1,0:T(8,128)(2,1)S(1)} copy-done((bf16[1,256,128]{2,1,0:T(8,128)(2,1)S(1)}, bf16[1,256,128]{2,1,0:T(8,128)(2,1)}, u32[]{:S(2)}) %copy-start) | copy-done | bytes 65560
  3.2 4.0 %collective-permute-start.3 = (bf16[512,128]{1,0:T(8,128)(2,1)S(1)}, bf16[512,128]{1,0:T(8,128)(2,1)S(1)}, u32[]{:S(2)}, u32[]{:S(2)}) collective-permute-start(bf16[512,128]{1,0:T(8,128)(2,1)S(1)} %shard_map.95.refs_2_), channel_id=1, source_target_pairs={{0,4},{1,3},{2,6},{3,1},{4,0},{5,7},{6,2},{7,5},{8,12},{9,11},{10,... | collective-permute-start | bytes 393224 | tf_op jit(solution)/shard_map/ppermute | solution.py:228
  7.1 1.2 %shard_map.96 = (bf16[512,128]{1,0:T(8,128)(2,1)S(1)}, bf16[800,128]{1,0:T(8,128)(2,1)S(1)}) custom-call(bf16[2,512,128]{2,1,0:T(8,128)(2,1)} %cols_ref.1, bf16[2,32,512]{2,1,0:T(8,128)(2,1)} %bitcast.41), custom_call_target="tpu_custom_call" | custom-call | tf_op jit(solution)/shard_map/pallas_call | solution.py:37
  8.4 1.6 %collective-permute-start.5 = (bf16[800,128]{1,0:T(8,128)(2,1)S(1)}, bf16[800,128]{1,0:T(8,128)(2,1)S(1)}, u32[]{:S(2)}, u32[]{:S(2)}) collective-permute-start(bf16[800,128]{1,0:T(8,128)(2,1)S(1)} %get-tuple-element.23.refs_7_), channel_id=1, source_target_pairs={{0,8},{8,0},{16,24},{24,16},{1,9},{9,1},{17,25},{25,17},{2,10},{10... | collective-permute-start | bytes 614408 | tf_op jit(solution)/shard_map/ppermute | solution.py:187
  9.9 1.5 %collective-permute-start.6 = (bf16[800,128]{1,0:T(8,128)(2,1)S(1)}, bf16[800,128]{1,0:T(8,128)(2,1)S(1)}, u32[]{:S(2)}, u32[]{:S(2)}) collective-permute-start(bf16[800,128]{1,0:T(8,128)(2,1)S(1)} %get-tuple-element.23.refs_7_), channel_id=1, source_target_pairs={{0,16},{8,24},{16,0},{24,8},{1,17},{9,25},{17,1},{25,9},{2,18},{10... | collective-permute-start | bytes 614408 | tf_op jit(solution)/shard_map/ppermute | solution.py:187
  11.4 0.5 %collective-permute-start.7 = (bf16[800,128]{1,0:T(8,128)(2,1)S(1)}, bf16[800,128]{1,0:T(8,128)(2,1)S(1)}, u32[]{:S(2)}, u32[]{:S(2)}) collective-permute-start(bf16[800,128]{1,0:T(8,128)(2,1)S(1)} %get-tuple-element.23.refs_7_), channel_id=1, source_target_pairs={{0,24},{8,16},{16,8},{24,0},{1,25},{9,17},{17,9},{25,1},{2,26},{10... | collective-permute-start | bytes 614408 | tf_op jit(solution)/shard_map/ppermute | solution.py:187
  11.9 1.3 %collective-permute-start.1 = (bf16[256,128]{1,0:T(8,128)(2,1)S(1)}, bf16[256,128]{1,0:T(8,128)(2,1)S(1)}, u32[]{:S(2)}, u32[]{:S(2)}) collective-permute-start(bf16[256,128]{1,0:T(8,128)(2,1)S(1)} %bitcast.36), channel_id=1, source_target_pairs={{0,6},{1,7},{2,4},{3,5},{4,2},{5,3},{6,0},{7,1},{8,14},{9,15},{10,... | collective-permute-start | bytes 196616 | tf_op jit(solution)/shard_map/ppermute | solution.py:228
  13.3 0.0 collective-permute-done.3.refs_5_
  13.3 0.0 collective-permute-start.4
  13.3 4.7 %collective-permute-done.1.refs_3_ = bf16[256,128]{1,0:T(8,128)(2,1)S(1)} collective-permute-done((bf16[256,128]{1,0:T(8,128)(2,1)S(1)}, bf16[256,128]{1,0:T(8,128)(2,1)S(1)}, u32[]{:S(2)}, u32[]{:S(2)}) %collective-permute-start.1) | collective-permute-done | bytes 65568 | tf_op jit(solution)/shard_map/ppermute | solution.py:228
  18.0 0.0 collective-permute-start.2
  18.0 1.8 %shard_map.94 = (bf16[2,64,2048]{2,1,0:T(8,128)(2,1)S(1)}, bf16[2,64,2048]{2,1,0:T(8,128)(2,1)S(1)}, bf16[64,2048]{1,0:T(8,128)(2,1)S(1)}, bf16[64,2048]{1,0:T(8...) custom-call(bf16[2,64,2048]{2,1,0:T(8,128)(2,1)} %bitcast.37, ...), custom_call_target="tpu_custom_call" | custom-call | tf_op jit(solution)/shard_map/pallas_call | solution.py:37
  19.8 0.0 collective-permute-done.2.refs_4_
  19.8 0.0 collective-permute-done.5.refs_8_
  19.8 0.1 collective-permute-done.6.refs_9_
  19.9 0.0 collective-permute-done.7.refs_10_
  19.9 0.0 collective-permute-done.4.refs_6_
  19.9 1.1 %shard_map.97 = (f32[64,128]{1,0:T(8,128)S(1)}, bf16[2048,128]{1,0:T(8,128)(2,1)S(1)}, f32[4,32,256]{2,1,0:T(8,128)S(1)}, bf16[4,32,256]{2,1,0:T(8,128)(2,1)S(1)}) custom-call(bf16[2,64,2048]{2,1,0:T(8,128)(2,1)S(1)} %get-tuple-element.17.refs_0_, bf16[2,64,2048]{2,1,0:T(8,128)(2,1)S(1)} %get-tuple-element.18.refs_1_, ...), custom_call_target="tpu_custom_call" | custom-call | tf_op jit(solution)/shard_map/pallas_call | solution.py:37
  21.1 0.5 %collective-permute-start.11 = (bf16[4,32,256]{2,1,0:T(8,128)(2,1)S(1)}, bf16[4,32,256]{2,1,0:T(8,128)(2,1)S(1)}, u32[]{:S(2)}, u32[]{:S(2)}) collective-permute-start(bf16[4,32,256]{2,1,0:T(8,128)(2,1)S(1)} %get-tuple-element.30), channel_id=1, source_target_pairs={{0,1},{1,0},{2,3},{3,2},{4,5},{5,4},{6,7},{7,6},{8,9},{9,8},{10,11... | collective-permute-start | bytes 196616 | tf_op jit(solution)/shard_map/ppermute | solution.py:187
  21.5 2.5 %collective-permute-start.10 = (bf16[512,128]{1,0:T(8,128)(2,1)S(1)}, bf16[512,128]{1,0:T(8,128)(2,1)S(1)}, u32[]{:S(2)}, u32[]{:S(2)}) collective-permute-start(bf16[512,128]{1,0:T(8,128)(2,1)S(1)} %get-tuple-element.26.refs_8_), channel_id=1, source_target_pairs={{0,24},{8,16},{16,8},{24,0},{1,25},{9,17},{17,9},{25,1},{2,26},{10... | collective-permute-start | bytes 393224 | tf_op jit(solution)/shard_map/ppermute | solution.py:187
  24.0 0.5 %collective-permute-start.8 = (bf16[512,128]{1,0:T(8,128)(2,1)S(1)}, bf16[512,128]{1,0:T(8,128)(2,1)S(1)}, u32[]{:S(2)}, u32[]{:S(2)}) collective-permute-start(bf16[512,128]{1,0:T(8,128)(2,1)S(1)} %get-tuple-element.26.refs_8_), channel_id=1, source_target_pairs={{0,8},{8,0},{16,24},{24,16},{1,9},{9,1},{17,25},{25,17},{2,10},{10... | collective-permute-start | bytes 393224 | tf_op jit(solution)/shard_map/ppermute | solution.py:187
  24.5 0.5 %collective-permute-start.9 = (bf16[512,128]{1,0:T(8,128)(2,1)S(1)}, bf16[512,128]{1,0:T(8,128)(2,1)S(1)}, u32[]{:S(2)}, u32[]{:S(2)}) collective-permute-start(bf16[512,128]{1,0:T(8,128)(2,1)S(1)} %get-tuple-element.26.refs_8_), channel_id=1, source_target_pairs={{0,16},{8,24},{16,0},{24,8},{1,17},{9,25},{17,1},{25,9},{2,18},{10... | collective-permute-start | bytes 393224 | tf_op jit(solution)/shard_map/ppermute | solution.py:187
  25.0 0.0 collective-permute-done.11
  25.0 0.3 collective-permute-start.12
  25.4 2.4 %collective-permute-start.13 = (bf16[32,256]{1,0:T(8,128)(2,1)S(1)}, bf16[32,256]{1,0:T(8,128)(2,1)S(1)}, u32[]{:S(2)}, u32[]{:S(2)}) collective-permute-start(bf16[32,256]{1,0:T(8,128)(2,1)S(1)} %get-tuple-element.33), channel_id=1, source_target_pairs={{0,4},{1,5},{2,6},{3,7},{4,0},{5,1},{6,2},{7,3},{8,12},{9,13},{10,... | collective-permute-start | bytes 49160 | tf_op jit(solution)/shard_map/ppermute | solution.py:187
  27.8 1.0 %collective-permute-done.10.refs_11_ = bf16[512,128]{1,0:T(8,128)(2,1)S(1)} collective-permute-done((bf16[512,128]{1,0:T(8,128)(2,1)S(1)}, bf16[512,128]{1,0:T(8,128)(2,1)S(1)}, u32[]{:S(2)}, u32[]{:S(2)}) %collective-permute-start.10) | collective-permute-done | bytes 131104 | tf_op jit(solution)/shard_map/ppermute | solution.py:187
  28.8 2.1 %collective-permute-start.14 = (bf16[32,256]{1,0:T(8,128)(2,1)S(1)}, bf16[32,256]{1,0:T(8,128)(2,1)S(1)}, u32[]{:S(2)}, u32[]{:S(2)}) collective-permute-start(bf16[32,256]{1,0:T(8,128)(2,1)S(1)} %get-tuple-element.32), channel_id=1, source_target_pairs={{0,6},{1,7},{2,4},{3,5},{4,2},{5,3},{6,0},{7,1},{8,14},{9,15},{10,... | collective-permute-start | bytes 49160 | tf_op jit(solution)/shard_map/ppermute | solution.py:187
  30.9 0.0 collective-permute-done.8.refs_9_
  30.9 0.0 collective-permute-done.9.refs_10_
  30.9 2.3 %shard_map.98 = (bf16[2,64,2048]{2,1,0:T(8,128)(2,1)}, bf16[2,64,2048]{2,1,0:T(8,128)(2,1)}) custom-call(bf16[2,64,2048]{2,1,0:T(8,128)(2,1)S(1)} %get-tuple-element.17.refs_0_, bf16[2,64,2048]{2,1,0:T(8,128)(2,1)S(1)} %get-tuple-element.18.refs_1_, bf16[64,2048]{1,0:T(8,128)(2,1)S(1)} %get-tuple-element.19.refs_2_, ...), custom_call_target="tpu_custom_call" | custom-call | tf_op jit(solution)/shard_map/pallas_call | solution.py:37
  33.2 0.0 collective-permute-done.12
  33.2 0.0 collective-permute-done.13
  33.2 1.1 %collective-permute-done.14 = bf16[32,256]{1,0:T(8,128)(2,1)S(1)} collective-permute-done((bf16[32,256]{1,0:T(8,128)(2,1)S(1)}, bf16[32,256]{1,0:T(8,128)(2,1)S(1)}, u32[]{:S(2)}, u32[]{:S(2)}) %collective-permute-start.14) | collective-permute-done | bytes 16416 | tf_op jit(solution)/shard_map/ppermute | solution.py:187
  34.3 0.6 %fusion.2 = f32[1,256,32]{1,2,0:T(8,128)} fusion(bf16[32,256]{1,0:T(8,128)(2,1)S(1)} %collective-permute-done.14, bf16[32,256]{1,0:T(8,128)(2,1)S(1)} %collective-permute-done.13, bf16[32,256]{1,0:T(8,128)(2,1)S(1)} %collective-permute-done.12, f32[4,32,256]{2,1,0:T(8,128)S(1)} %get-tuple-element.29, bf16[4,32,256]{2,1,0:T(8,128)(2,1)S(1)} %collective-permute-done.11), kind=kLoop, calls=%fused_computation.3 | loop fusion | flops 65536 | bytes 131072 | tf_op jit(solution)/shard_map/broadcast_in_dim | solution.py:282
  (2 shorter events, 0.0 us)
Async XLA Ops:
  0.6 1.7 %collective-permute-start = (bf16[256,128]{1,0:T(8,128)(2,1)}, bf16[256,128]{1,0:T(8,128)(2,1)S(1)}, u32[]{:S(2)}, u32[]{:S(2)}) collective-permute-start(bf16[256,128]{1,0:T(8,128)(2,1)} %bitcast.34), channel_id=1, source_target_pairs={{0,1},{1,0},{2,3},{3,2},{4,5},{5,4},{6,7},{7,6},{8,9},{9,8},{10,11... | collective-permute-start | bytes 196616 | tf_op jit(solution)/shard_map/ppermute | solution.py:187
  2.3 0.8 %copy-start = (bf16[1,256,128]{2,1,0:T(8,128)(2,1)S(1)}, bf16[1,256,128]{2,1,0:T(8,128)(2,1)}, u32[]{:S(2)}) copy-start(bf16[1,256,128]{2,1,0:T(8,128)(2,1)} %param.9) | copy-start | bytes 196612
  3.2 10.1 %collective-permute-start.3 = (bf16[512,128]{1,0:T(8,128)(2,1)S(1)}, bf16[512,128]{1,0:T(8,128)(2,1)S(1)}, u32[]{:S(2)}, u32[]{:S(2)}) collective-permute-start(bf16[512,128]{1,0:T(8,128)(2,1)S(1)} %shard_map.95.refs_2_), channel_id=1, source_target_pairs={{0,4},{1,3},{2,6},{3,1},{4,0},{5,7},{6,2},{7,5},{8,12},{9,11},{10,... | collective-permute-start | bytes 393224 | tf_op jit(solution)/shard_map/ppermute | solution.py:228
  8.4 11.4 %collective-permute-start.5 = (bf16[800,128]{1,0:T(8,128)(2,1)S(1)}, bf16[800,128]{1,0:T(8,128)(2,1)S(1)}, u32[]{:S(2)}, u32[]{:S(2)}) collective-permute-start(bf16[800,128]{1,0:T(8,128)(2,1)S(1)} %get-tuple-element.23.refs_7_), channel_id=1, source_target_pairs={{0,8},{8,0},{16,24},{24,16},{1,9},{9,1},{17,25},{25,17},{2,10},{10... | collective-permute-start | bytes 614408 | tf_op jit(solution)/shard_map/ppermute | solution.py:187
  9.9 10.0 %collective-permute-start.6 = (bf16[800,128]{1,0:T(8,128)(2,1)S(1)}, bf16[800,128]{1,0:T(8,128)(2,1)S(1)}, u32[]{:S(2)}, u32[]{:S(2)}) collective-permute-start(bf16[800,128]{1,0:T(8,128)(2,1)S(1)} %get-tuple-element.23.refs_7_), channel_id=1, source_target_pairs={{0,16},{8,24},{16,0},{24,8},{1,17},{9,25},{17,1},{25,9},{2,18},{10... | collective-permute-start | bytes 614408 | tf_op jit(solution)/shard_map/ppermute | solution.py:187
  11.4 8.5 %collective-permute-start.7 = (bf16[800,128]{1,0:T(8,128)(2,1)S(1)}, bf16[800,128]{1,0:T(8,128)(2,1)S(1)}, u32[]{:S(2)}, u32[]{:S(2)}) collective-permute-start(bf16[800,128]{1,0:T(8,128)(2,1)S(1)} %get-tuple-element.23.refs_7_), channel_id=1, source_target_pairs={{0,24},{8,16},{16,8},{24,0},{1,25},{9,17},{17,9},{25,1},{2,26},{10... | collective-permute-start | bytes 614408 | tf_op jit(solution)/shard_map/ppermute | solution.py:187
  11.9 6.1 %collective-permute-start.1 = (bf16[256,128]{1,0:T(8,128)(2,1)S(1)}, bf16[256,128]{1,0:T(8,128)(2,1)S(1)}, u32[]{:S(2)}, u32[]{:S(2)}) collective-permute-start(bf16[256,128]{1,0:T(8,128)(2,1)S(1)} %bitcast.36), channel_id=1, source_target_pairs={{0,6},{1,7},{2,4},{3,5},{4,2},{5,3},{6,0},{7,1},{8,14},{9,15},{10,... | collective-permute-start | bytes 196616 | tf_op jit(solution)/shard_map/ppermute | solution.py:228
  13.3 6.7 %collective-permute-start.4 = (bf16[512,128]{1,0:T(8,128)(2,1)S(1)}, bf16[512,128]{1,0:T(8,128)(2,1)S(1)}, u32[]{:S(2)}, u32[]{:S(2)}) collective-permute-start(bf16[512,128]{1,0:T(8,128)(2,1)S(1)} %collective-permute-done.3.refs_5_), channel_id=1, source_target_pairs={{0,1},{1,0},{2,3},{3,2},{4,5},{5,4},{6,7},{7,6},{8,9},{9,8},{10,11... | collective-permute-start | bytes 393224 | tf_op jit(solution)/shard_map/ppermute | solution.py:187
  18.0 1.8 %collective-permute-start.2 = (bf16[256,128]{1,0:T(8,128)(2,1)S(1)}, bf16[256,128]{1,0:T(8,128)(2,1)S(1)}, u32[]{:S(2)}, u32[]{:S(2)}) collective-permute-start(bf16[256,128]{1,0:T(8,128)(2,1)S(1)} %collective-permute-done.1.refs_3_), channel_id=1, source_target_pairs={{0,1},{1,0},{2,3},{3,2},{4,5},{5,4},{6,7},{7,6},{8,9},{9,8},{10,11... | collective-permute-start | bytes 196616 | tf_op jit(solution)/shard_map/ppermute | solution.py:187
  21.1 4.0 %collective-permute-start.11 = (bf16[4,32,256]{2,1,0:T(8,128)(2,1)S(1)}, bf16[4,32,256]{2,1,0:T(8,128)(2,1)S(1)}, u32[]{:S(2)}, u32[]{:S(2)}) collective-permute-start(bf16[4,32,256]{2,1,0:T(8,128)(2,1)S(1)} %get-tuple-element.30), channel_id=1, source_target_pairs={{0,1},{1,0},{2,3},{3,2},{4,5},{5,4},{6,7},{7,6},{8,9},{9,8},{10,11... | collective-permute-start | bytes 196616 | tf_op jit(solution)/shard_map/ppermute | solution.py:187
  21.5 7.3 %collective-permute-start.10 = (bf16[512,128]{1,0:T(8,128)(2,1)S(1)}, bf16[512,128]{1,0:T(8,128)(2,1)S(1)}, u32[]{:S(2)}, u32[]{:S(2)}) collective-permute-start(bf16[512,128]{1,0:T(8,128)(2,1)S(1)} %get-tuple-element.26.refs_8_), channel_id=1, source_target_pairs={{0,24},{8,16},{16,8},{24,0},{1,25},{9,17},{17,9},{25,1},{2,26},{10... | collective-permute-start | bytes 393224 | tf_op jit(solution)/shard_map/ppermute | solution.py:187
  24.0 6.9 %collective-permute-start.8 = (bf16[512,128]{1,0:T(8,128)(2,1)S(1)}, bf16[512,128]{1,0:T(8,128)(2,1)S(1)}, u32[]{:S(2)}, u32[]{:S(2)}) collective-permute-start(bf16[512,128]{1,0:T(8,128)(2,1)S(1)} %get-tuple-element.26.refs_8_), channel_id=1, source_target_pairs={{0,8},{8,0},{16,24},{24,16},{1,9},{9,1},{17,25},{25,17},{2,10},{10... | collective-permute-start | bytes 393224 | tf_op jit(solution)/shard_map/ppermute | solution.py:187
  24.5 6.4 %collective-permute-start.9 = (bf16[512,128]{1,0:T(8,128)(2,1)S(1)}, bf16[512,128]{1,0:T(8,128)(2,1)S(1)}, u32[]{:S(2)}, u32[]{:S(2)}) collective-permute-start(bf16[512,128]{1,0:T(8,128)(2,1)S(1)} %get-tuple-element.26.refs_8_), channel_id=1, source_target_pairs={{0,16},{8,24},{16,0},{24,8},{1,17},{9,25},{17,1},{25,9},{2,18},{10... | collective-permute-start | bytes 393224 | tf_op jit(solution)/shard_map/ppermute | solution.py:187
  25.0 8.2 %collective-permute-start.12 = (bf16[32,256]{1,0:T(8,128)(2,1)S(1)}, bf16[32,256]{1,0:T(8,128)(2,1)S(1)}, u32[]{:S(2)}, u32[]{:S(2)}) collective-permute-start(bf16[32,256]{1,0:T(8,128)(2,1)S(1)} %get-tuple-element.31), channel_id=1, source_target_pairs={{0,2},{1,3},{2,0},{3,1},{4,6},{5,7},{6,4},{7,5},{8,10},{9,11},{10,... | collective-permute-start | bytes 49160 | tf_op jit(solution)/shard_map/ppermute | solution.py:187
  25.4 7.8 %collective-permute-start.13 = (bf16[32,256]{1,0:T(8,128)(2,1)S(1)}, bf16[32,256]{1,0:T(8,128)(2,1)S(1)}, u32[]{:S(2)}, u32[]{:S(2)}) collective-permute-start(bf16[32,256]{1,0:T(8,128)(2,1)S(1)} %get-tuple-element.33), channel_id=1, source_target_pairs={{0,4},{1,5},{2,6},{3,7},{4,0},{5,1},{6,2},{7,3},{8,12},{9,13},{10,... | collective-permute-start | bytes 49160 | tf_op jit(solution)/shard_map/ppermute | solution.py:187
  28.8 5.5 %collective-permute-start.14 = (bf16[32,256]{1,0:T(8,128)(2,1)S(1)}, bf16[32,256]{1,0:T(8,128)(2,1)S(1)}, u32[]{:S(2)}, u32[]{:S(2)}) collective-permute-start(bf16[32,256]{1,0:T(8,128)(2,1)S(1)} %get-tuple-element.32), channel_id=1, source_target_pairs={{0,6},{1,7},{2,4},{3,5},{4,2},{5,3},{6,0},{7,1},{8,14},{9,15},{10,... | collective-permute-start | bytes 49160 | tf_op jit(solution)/shard_map/ppermute | solution.py:187
where the time goes:
time: 35.2 us; the launch traced here: 35 us
  starting transfers between devices  18.2 us (52%)
  waiting for transfers between devices  8.15 us (23%)
  Pallas kernels  6.44 us (18%)
  local copies, waits for them, and re-layouts  0.84 us (2%)
  between operations  0.69 us (2%)
  other arithmetic  0.64 us (2%)
    ppermute x13, starting transfers between devices, swap(): return lax.ppermute(value, axis, [(i, i ^ m) for i in range(count)])  12.9 us
    pallas_call x5, Pallas kernels, call(): pl.pallas_call(kernel, out_shape=out_shape, in_specs=[anywhere if k in ra...  6.44 us
    ppermute x2, starting transfers between devices, local(): got = lax.ppermute(rows if one == two else both, 'col', perm)  5.34 us
    ppermute x2, waiting for transfers between devices, local(): got = lax.ppermute(rows if one == two else both, 'col', perm)  4.71 us
    ppermute x13, waiting for transfers between devices, swap(): return lax.ppermute(value, axis, [(i, i ^ m) for i in range(count)])  3.44 us
    unnamed x2, local copies, waits for them, and re-layouts  0.84 us
  transfers between devices with their start and end apart: 15, of which 5 were waited for; matrix products, arithmetic and copies ran while one was open for 0% of the time, Pallas kernels for 15%

commit v1 on v0

--- a/solution.py
+++ b/solution.py
@@ -67,8 +67,8 @@
     v_ref[base:] = jnp.concatenate(part, axis=1).astype(BF16)
 
 
-def load_kernel(tiles, *refs):
-    sources, targets, (coef_a, coef_c), sems = refs[:4], refs[4:8], refs[8:10], refs[10]
+def load_kernel(*refs):
+    sources, targets, sems = refs[:4], refs[4:8], refs[8]
     copies = [
         pltpu.make_async_copy(s, t, sems.at[k]) for k, (s, t) in enumerate(zip(sources, targets))
     ]
@@ -76,7 +76,9 @@
         copy.start()
     for copy in copies:
         copy.wait()
-    left, right, omega, psi = targets
+
+
+def coef_kernel(tiles, left, right, omega, psi, coef_a, coef_c):
     for t in range(tiles):
         coef_a[t] = nt(omega[...], right[t]).astype(BF16)
         coef_c[t] = nt(psi[...], left[t]).astype(BF16)
@@ -210,13 +212,20 @@
         hbm=(0, 1),
     )
     sources = (left, right, omega_t, psi_t)
-    left, right, omega_t, psi_t, coef_a, coef_c = call(
-        functools.partial(load_kernel, tiles),
-        tuple(vmem(x.shape, BF16) for x in sources)
-        + (vmem((tiles, wide, rank), BF16), vmem((tiles, wide, rank), BF16)),
+    left, right, omega_t, psi_t = call(
+        load_kernel,
+        tuple(vmem(x.shape, BF16) for x in sources),
         *sources,
         raw=(0, 1, 2, 3),
         scratch=[pltpu.SemaphoreType.DMA((4,))],
+    )
+    coef_a, coef_c = call(
+        functools.partial(coef_kernel, tiles),
+        (vmem((tiles, wide, rank), BF16), vmem((tiles, wide, rank), BF16)),
+        left,
+        right,
+        omega_t,
+        psi_t,
     )
     vs = [v] + [row_swap(v, k) for k in range(1, n_row)]
     us = [u] + [row_swap(u, k) for k in range(1, n_row)]

time: 35.2 us -> 34.8 us (0.989)
  waiting for transfers between devices: 8.15 us -> 7.5 us
    ppermute x13, waiting for transfers between devices: 3.44 us -> 2.79 us  [swap(): return lax.ppermute(value, axis, [(i, i ^ m) for i in range(count)])]
    pallas_call x5 -> x6, Pallas kernels: 6.44 us -> 6.42 us  [call(): pl.pallas_call(kernel, out_shape=out_shape, in_specs=[anywhere if k in ra...]
where the time goes in v1:
time: 34.8 us; the launch traced here: 34.6 us
  starting transfers between devices  18.5 us (53%)
  waiting for transfers between devices  7.5 us (22%)
  Pallas kernels  6.42 us (18%)
  local copies, waits for them, and re-layouts  0.84 us (2%)
  between operations  0.71 us (2%)
  other arithmetic  0.64 us (2%)
    ppermute x13, starting transfers between devices, swap(): return lax.ppermute(value, axis, [(i, i ^ m) for i in range(count)])  13.2 us
    pallas_call x6, Pallas kernels, call(): pl.pallas_call(kernel, out_shape=out_shape, in_specs=[anywhere if k in ra...  6.42 us
    ppermute x2, starting transfers between devices, local(): got = lax.ppermute(rows if one == two else both, 'col', perm)  5.34 us
    ppermute x2, waiting for transfers between devices, local(): got = lax.ppermute(rows if one == two else both, 'col', perm)  4.71 us
    ppermute x13, waiting for transfers between devices, swap(): return lax.ppermute(value, axis, [(i, i ^ m) for i in range(count)])  2.79 us
    unnamed x2, local copies, waits for them, and re-layouts  0.84 us
  transfers between devices with their start and end apart: 15, of which 5 were waited for; matrix products, arithmetic and copies ran while one was open for 0% of the time, Pallas kernels for 15%

profile of v1, /device:TPU:0, one launch (start us, length us, event | category | flops | bytes accessed | tf_op | source)
XLA Modules:
  0.0 34.6 jit_solution(6568733284882979898)
XLA Ops:
  0.6 0.6 %collective-permute-start = (bf16[256,128]{1,0:T(8,128)(2,1)}, bf16[256,128]{1,0:T(8,128)(2,1)S(1)}, u32[]{:S(2)}, u32[]{:S(2)}) collective-permute-start(bf16[256,128]{1,0:T(8,128)(2,1)} %bitcast.34), channel_id=1, source_target_pairs={{0,1},{1,0},{2,3},{3,2},{4,5},{5,4},{6,7},{7,6},{8,9},{9,8},{10,11... | collective-permute-start | bytes 196616 | tf_op jit(solution)/shard_map/ppermute | solution.py:189
  1.2 1.1 %collective-permute-done.other = bf16[256,128]{1,0:T(8,128)(2,1)S(1)} collective-permute-done((bf16[256,128]{1,0:T(8,128)(2,1)}, bf16[256,128]{1,0:T(8,128)(2,1)S(1)}, u32[]{:S(2)}, u32[]{:S(2)}) %collective-permute-start) | collective-permute-done | bytes 65568 | tf_op jit(solution)/shard_map/ppermute | solution.py:189
  2.3 0.0 copy-start
  2.3 0.8 %copy-done = bf16[1,256,128]{2,1,0:T(8,128)(2,1)S(1)} copy-done((bf16[1,256,128]{2,1,0:T(8,128)(2,1)S(1)}, bf16[1,256,128]{2,1,0:T(8,128)(2,1)}, u32[]{:S(2)}) %copy-start) | copy-done | bytes 65560
  3.2 4.0 %collective-permute-start.3 = (bf16[512,128]{1,0:T(8,128)(2,1)S(1)}, bf16[512,128]{1,0:T(8,128)(2,1)S(1)}, u32[]{:S(2)}, u32[]{:S(2)}) collective-permute-start(bf16[512,128]{1,0:T(8,128)(2,1)S(1)} %shard_map.96.refs_2_), channel_id=1, source_target_pairs={{0,4},{1,3},{2,6},{3,1},{4,0},{5,7},{6,2},{7,5},{8,12},{9,11},{10,... | collective-permute-start | bytes 393224 | tf_op jit(solution)/shard_map/ppermute | solution.py:237
  7.1 1.2 %shard_map.97 = (bf16[512,128]{1,0:T(8,128)(2,1)S(1)}, bf16[800,128]{1,0:T(8,128)(2,1)S(1)}) custom-call(bf16[2,512,128]{2,1,0:T(8,128)(2,1)} %cols_ref.1, bf16[2,32,512]{2,1,0:T(8,128)(2,1)} %bitcast.41), custom_call_target="tpu_custom_call" | custom-call | tf_op jit(solution)/shard_map/pallas_call | solution.py:37
  8.4 1.6 %collective-permute-start.5 = (bf16[800,128]{1,0:T(8,128)(2,1)S(1)}, bf16[800,128]{1,0:T(8,128)(2,1)S(1)}, u32[]{:S(2)}, u32[]{:S(2)}) collective-permute-start(bf16[800,128]{1,0:T(8,128)(2,1)S(1)} %get-tuple-element.23.refs_7_), channel_id=1, source_target_pairs={{0,8},{8,0},{16,24},{24,16},{1,9},{9,1},{17,25},{25,17},{2,10},{10... | collective-permute-start | bytes 614408 | tf_op jit(solution)/shard_map/ppermute | solution.py:189
  9.9 1.5 %collective-permute-start.6 = (bf16[800,128]{1,0:T(8,128)(2,1)S(1)}, bf16[800,128]{1,0:T(8,128)(2,1)S(1)}, u32[]{:S(2)}, u32[]{:S(2)}) collective-permute-start(bf16[800,128]{1,0:T(8,128)(2,1)S(1)} %get-tuple-element.23.refs_7_), channel_id=1, source_target_pairs={{0,16},{8,24},{16,0},{24,8},{1,17},{9,25},{17,1},{25,9},{2,18},{10... | collective-permute-start | bytes 614408 | tf_op jit(solution)/shard_map/ppermute | solution.py:189
  11.4 0.5 %collective-permute-start.7 = (bf16[800,128]{1,0:T(8,128)(2,1)S(1)}, bf16[800,128]{1,0:T(8,128)(2,1)S(1)}, u32[]{:S(2)}, u32[]{:S(2)}) collective-permute-start(bf16[800,128]{1,0:T(8,128)(2,1)S(1)} %get-tuple-element.23.refs_7_), channel_id=1, source_target_pairs={{0,24},{8,16},{16,8},{24,0},{1,25},{9,17},{17,9},{25,1},{2,26},{10... | collective-permute-start | bytes 614408 | tf_op jit(solution)/shard_map/ppermute | solution.py:189
  11.9 1.3 %collective-permute-start.1 = (bf16[256,128]{1,0:T(8,128)(2,1)S(1)}, bf16[256,128]{1,0:T(8,128)(2,1)S(1)}, u32[]{:S(2)}, u32[]{:S(2)}) collective-permute-start(bf16[256,128]{1,0:T(8,128)(2,1)S(1)} %bitcast.36), channel_id=1, source_target_pairs={{0,6},{1,7},{2,4},{3,5},{4,2},{5,3},{6,0},{7,1},{8,14},{9,15},{10,... | collective-permute-start | bytes 196616 | tf_op jit(solution)/shard_map/ppermute | solution.py:237
  13.3 0.0 collective-permute-done.3.refs_5_
  13.3 0.0 collective-permute-start.4
  13.3 4.7 %collective-permute-done.1.refs_3_ = bf16[256,128]{1,0:T(8,128)(2,1)S(1)} collective-permute-done((bf16[256,128]{1,0:T(8,128)(2,1)S(1)}, bf16[256,128]{1,0:T(8,128)(2,1)S(1)}, u32[]{:S(2)}, u32[]{:S(2)}) %collective-permute-start.1) | collective-permute-done | bytes 65568 | tf_op jit(solution)/shard_map/ppermute | solution.py:237
  18.0 0.0 collective-permute-start.2
  18.0 1.4 %shard_map.94 = (bf16[2,64,2048]{2,1,0:T(8,128)(2,1)S(1)}, bf16[2,64,2048]{2,1,0:T(8,128)(2,1)S(1)}, bf16[64,2048]{1,0:T(8,128)(2,1)S(1)}, bf16[64,2048]{1,0:T(8,128)(2,1)S(1)}) custom-call(bf16[2,64,2048]{2,1,0:T(8,128)(2,1)} %bitcast.37, bf16[2,64,2048]{2,1,0:T(8,128)(2,1)} %bitcast.38, bf16[64,2048]{1,0:T(8,128)(2,1)} %bitcast.39, bf16[64,2048]{1,0:T(8,128)(2,1)} %bitcast.40), custom_call_target="tpu_custom_call" | custom-call | tf_op jit(solution)/shard_map/pallas_call | solution.py:37
  19.4 0.0 collective-permute-done.2.refs_4_
  19.4 0.0 collective-permute-done.5.refs_8_
  19.4 0.6 %collective-permute-done.6.refs_9_ = bf16[800,128]{1,0:T(8,128)(2,1)S(1)} collective-permute-done((bf16[800,128]{1,0:T(8,128)(2,1)S(1)}, bf16[800,128]{1,0:T(8,128)(2,1)S(1)}, u32[]{:S(2)}, u32[]{:S(2)}) %collective-permute-start.6) | collective-permute-done | bytes 204832 | tf_op jit(solution)/shard_map/ppermute | solution.py:189
  19.9 0.0 collective-permute-done.7.refs_10_
  19.9 0.0 collective-permute-done.4.refs_6_
  19.9 1.1 %shard_map.98 = (f32[64,128]{1,0:T(8,128)S(1)}, bf16[2048,128]{1,0:T(8,128)(2,1)S(1)}, f32[4,32,256]{2,1,0:T(8,128)S(1)}, bf16[4,32,256]{2,1,0:T(8,128)(2,1)S(1)}) custom-call(bf16[2,64,2048]{2,1,0:T(8,128)(2,1)S(1)} %get-tuple-element.17.left.refs_0_, bf16[2,64,2048]{2,1,0:T(8,128)(2,1)S(1)} %get-tuple-element.18.right.refs_1_, ...), custom_call_target="tpu_custom_call" | custom-call | tf_op jit(solution)/shard_map/pallas_call | solution.py:37
  21.1 0.1 collective-permute-start.11
  21.1 2.4 %collective-permute-start.10 = (bf16[512,128]{1,0:T(8,128)(2,1)S(1)}, bf16[512,128]{1,0:T(8,128)(2,1)S(1)}, u32[]{:S(2)}, u32[]{:S(2)}) collective-permute-start(bf16[512,128]{1,0:T(8,128)(2,1)S(1)} %get-tuple-element.26.refs_8_), channel_id=1, source_target_pairs={{0,24},{8,16},{16,8},{24,0},{1,25},{9,17},{17,9},{25,1},{2,26},{10... | collective-permute-start | bytes 393224 | tf_op jit(solution)/shard_map/ppermute | solution.py:189
  23.6 0.6 %collective-permute-start.8 = (bf16[512,128]{1,0:T(8,128)(2,1)S(1)}, bf16[512,128]{1,0:T(8,128)(2,1)S(1)}, u32[]{:S(2)}, u32[]{:S(2)}) collective-permute-start(bf16[512,128]{1,0:T(8,128)(2,1)S(1)} %get-tuple-element.26.refs_8_), channel_id=1, source_target_pairs={{0,8},{8,0},{16,24},{24,16},{1,9},{9,1},{17,25},{25,17},{2,10},{10... | collective-permute-start | bytes 393224 | tf_op jit(solution)/shard_map/ppermute | solution.py:189
  24.1 0.6 %collective-permute-start.9 = (bf16[512,128]{1,0:T(8,128)(2,1)S(1)}, bf16[512,128]{1,0:T(8,128)(2,1)S(1)}, u32[]{:S(2)}, u32[]{:S(2)}) collective-permute-start(bf16[512,128]{1,0:T(8,128)(2,1)S(1)} %get-tuple-element.26.refs_8_), channel_id=1, source_target_pairs={{0,16},{8,24},{16,0},{24,8},{1,17},{9,25},{17,1},{25,9},{2,18},{10... | collective-permute-start | bytes 393224 | tf_op jit(solution)/shard_map/ppermute | solution.py:189
  24.7 0.0 collective-permute-done.11
  24.7 0.7 %collective-permute-start.12 = (bf16[32,256]{1,0:T(8,128)(2,1)S(1)}, bf16[32,256]{1,0:T(8,128)(2,1)S(1)}, u32[]{:S(2)}, u32[]{:S(2)}) collective-permute-start(bf16[32,256]{1,0:T(8,128)(2,1)S(1)} %get-tuple-element.31), channel_id=1, source_target_pairs={{0,2},{1,3},{2,0},{3,1},{4,6},{5,7},{6,4},{7,5},{8,10},{9,11},{10,... | collective-permute-start | bytes 49160 | tf_op jit(solution)/shard_map/ppermute | solution.py:189
  25.4 2.4 %collective-permute-start.13 = (bf16[32,256]{1,0:T(8,128)(2,1)S(1)}, bf16[32,256]{1,0:T(8,128)(2,1)S(1)}, u32[]{:S(2)}, u32[]{:S(2)}) collective-permute-start(bf16[32,256]{1,0:T(8,128)(2,1)S(1)} %get-tuple-element.33), channel_id=1, source_target_pairs={{0,4},{1,5},{2,6},{3,7},{4,0},{5,1},{6,2},{7,3},{8,12},{9,13},{10,... | collective-permute-start | bytes 49160 | tf_op jit(solution)/shard_map/ppermute | solution.py:189
  27.8 0.7 %collective-permute-done.10.refs_11_ = bf16[512,128]{1,0:T(8,128)(2,1)S(1)} collective-permute-done((bf16[512,128]{1,0:T(8,128)(2,1)S(1)}, bf16[512,128]{1,0:T(8,128)(2,1)S(1)}, u32[]{:S(2)}, u32[]{:S(2)}) %collective-permute-start.10) | collective-permute-done | bytes 131104 | tf_op jit(solution)/shard_map/ppermute | solution.py:189
  28.5 2.4 %collective-permute-start.14 = (bf16[32,256]{1,0:T(8,128)(2,1)S(1)}, bf16[32,256]{1,0:T(8,128)(2,1)S(1)}, u32[]{:S(2)}, u32[]{:S(2)}) collective-permute-start(bf16[32,256]{1,0:T(8,128)(2,1)S(1)} %get-tuple-element.32), channel_id=1, source_target_pairs={{0,6},{1,7},{2,4},{3,5},{4,2},{5,3},{6,0},{7,1},{8,14},{9,15},{10,... | collective-permute-start | bytes 49160 | tf_op jit(solution)/shard_map/ppermute | solution.py:189
  30.9 0.4 %shard_map.95 = (bf16[2,64,64]{2,1,0:T(8,128)(2,1)S(1)}, bf16[2,64,64]{2,1,0:T(8,128)(2,1)S(1)}) custom-call(bf16[2,64,2048]{2,1,0:T(8,128)(2,1)S(1)} %get-tuple-element.17.left.refs_0_, bf16[2,64,2048]{2,1,0:T(8,128)(2,1)S(1)} %get-tuple-element.18.right.refs_1_, bf16[64,2048]{1,0:T(8,128)(2,1)S(1)} %get-tuple-element.19.omega.refs_2_, ...), custom_call_target="tpu_custom_call" | custom-call | tf_op jit(solution)/shard_map/pallas_call | solution.py:37
  31.3 0.0 collective-permute-done.8.refs_9_
  31.3 0.0 collective-permute-done.9.refs_10_
  31.3 2.3 %shard_map.99 = (bf16[2,64,2048]{2,1,0:T(8,128)(2,1)}, bf16[2,64,2048]{2,1,0:T(8,128)(2,1)}) custom-call(bf16[2,64,2048]{2,1,0:T(8,128)(2,1)S(1)} %get-tuple-element.17.left.refs_0_, bf16[2,64,2048]{2,1,0:T(8,128)(2,1)S(1)} %get-tuple-element.18.right.refs_1_, bf16[64,2048]{1,0:T(8,128)(2,1)S(1)} %get-tuple-element.19.omega.refs_2_, ...), custom_call_target="tpu_custom_call" | custom-call | tf_op jit(solution)/shard_map/pallas_call | solution.py:37
  33.6 0.0 collective-permute-done.12
  33.6 0.0 collective-permute-done.13
  33.6 0.4 %collective-permute-done.14 = bf16[32,256]{1,0:T(8,128)(2,1)S(1)} collective-permute-done((bf16[32,256]{1,0:T(8,128)(2,1)S(1)}, bf16[32,256]{1,0:T(8,128)(2,1)S(1)}, u32[]{:S(2)}, u32[]{:S(2)}) %collective-permute-start.14) | collective-permute-done | bytes 16416 | tf_op jit(solution)/shard_map/ppermute | solution.py:189
  34.0 0.6 %fusion.2 = f32[1,256,32]{1,2,0:T(8,128)} fusion(bf16[32,256]{1,0:T(8,128)(2,1)S(1)} %collective-permute-done.14, bf16[32,256]{1,0:T(8,128)(2,1)S(1)} %collective-permute-done.13, bf16[32,256]{1,0:T(8,128)(2,1)S(1)} %collective-permute-done.12, f32[4,32,256]{2,1,0:T(8,128)S(1)} %get-tuple-element.29, bf16[4,32,256]{2,1,0:T(8,128)(2,1)S(1)} %collective-permute-done.11), kind=kLoop, calls=%fused_computation.3 | loop fusion | flops 65536 | bytes 131072 | tf_op jit(solution)/shard_map/broadcast_in_dim | solution.py:291
  (2 shorter events, 0.0 us)
Async XLA Ops:
  0.6 1.7 %collective-permute-start = (bf16[256,128]{1,0:T(8,128)(2,1)}, bf16[256,128]{1,0:T(8,128)(2,1)S(1)}, u32[]{:S(2)}, u32[]{:S(2)}) collective-permute-start(bf16[256,128]{1,0:T(8,128)(2,1)} %bitcast.34), channel_id=1, source_target_pairs={{0,1},{1,0},{2,3},{3,2},{4,5},{5,4},{6,7},{7,6},{8,9},{9,8},{10,11... | collective-permute-start | bytes 196616 | tf_op jit(solution)/shard_map/ppermute | solution.py:189
  2.3 0.8 %copy-start = (bf16[1,256,128]{2,1,0:T(8,128)(2,1)S(1)}, bf16[1,256,128]{2,1,0:T(8,128)(2,1)}, u32[]{:S(2)}) copy-start(bf16[1,256,128]{2,1,0:T(8,128)(2,1)} %param.9) | copy-start | bytes 196612
  3.2 10.1 %collective-permute-start.3 = (bf16[512,128]{1,0:T(8,128)(2,1)S(1)}, bf16[512,128]{1,0:T(8,128)(2,1)S(1)}, u32[]{:S(2)}, u32[]{:S(2)}) collective-permute-start(bf16[512,128]{1,0:T(8,128)(2,1)S(1)} %shard_map.96.refs_2_), channel_id=1, source_target_pairs={{0,4},{1,3},{2,6},{3,1},{4,0},{5,7},{6,2},{7,5},{8,12},{9,11},{10,... | collective-permute-start | bytes 393224 | tf_op jit(solution)/shard_map/ppermute | solution.py:237
  8.4 11.0 %collective-permute-start.5 = (bf16[800,128]{1,0:T(8,128)(2,1)S(1)}, bf16[800,128]{1,0:T(8,128)(2,1)S(1)}, u32[]{:S(2)}, u32[]{:S(2)}) collective-permute-start(bf16[800,128]{1,0:T(8,128)(2,1)S(1)} %get-tuple-element.23.refs_7_), channel_id=1, source_target_pairs={{0,8},{8,0},{16,24},{24,16},{1,9},{9,1},{17,25},{25,17},{2,10},{10... | collective-permute-start | bytes 614408 | tf_op jit(solution)/shard_map/ppermute | solution.py:189
  9.9 10.0 %collective-permute-start.6 = (bf16[800,128]{1,0:T(8,128)(2,1)S(1)}, bf16[800,128]{1,0:T(8,128)(2,1)S(1)}, u32[]{:S(2)}, u32[]{:S(2)}) collective-permute-start(bf16[800,128]{1,0:T(8,128)(2,1)S(1)} %get-tuple-element.23.refs_7_), channel_id=1, source_target_pairs={{0,16},{8,24},{16,0},{24,8},{1,17},{9,25},{17,1},{25,9},{2,18},{10... | collective-permute-start | bytes 614408 | tf_op jit(solution)/shard_map/ppermute | solution.py:189
  11.4 8.5 %collective-permute-start.7 = (bf16[800,128]{1,0:T(8,128)(2,1)S(1)}, bf16[800,128]{1,0:T(8,128)(2,1)S(1)}, u32[]{:S(2)}, u32[]{:S(2)}) collective-permute-start(bf16[800,128]{1,0:T(8,128)(2,1)S(1)} %get-tuple-element.23.refs_7_), channel_id=1, source_target_pairs={{0,24},{8,16},{16,8},{24,0},{1,25},{9,17},{17,9},{25,1},{2,26},{10... | collective-permute-start | bytes 614408 | tf_op jit(solution)/shard_map/ppermute | solution.py:189
  11.9 6.1 %collective-permute-start.1 = (bf16[256,128]{1,0:T(8,128)(2,1)S(1)}, bf16[256,128]{1,0:T(8,128)(2,1)S(1)}, u32[]{:S(2)}, u32[]{:S(2)}) collective-permute-start(bf16[256,128]{1,0:T(8,128)(2,1)S(1)} %bitcast.36), channel_id=1, source_target_pairs={{0,6},{1,7},{2,4},{3,5},{4,2},{5,3},{6,0},{7,1},{8,14},{9,15},{10,... | collective-permute-start | bytes 196616 | tf_op jit(solution)/shard_map/ppermute | solution.py:237
  13.3 6.7 %collective-permute-start.4 = (bf16[512,128]{1,0:T(8,128)(2,1)S(1)}, bf16[512,128]{1,0:T(8,128)(2,1)S(1)}, u32[]{:S(2)}, u32[]{:S(2)}) collective-permute-start(bf16[512,128]{1,0:T(8,128)(2,1)S(1)} %collective-permute-done.3.refs_5_), channel_id=1, source_target_pairs={{0,1},{1,0},{2,3},{3,2},{4,5},{5,4},{6,7},{7,6},{8,9},{9,8},{10,11... | collective-permute-start | bytes 393224 | tf_op jit(solution)/shard_map/ppermute | solution.py:189
  18.0 1.4 %collective-permute-start.2 = (bf16[256,128]{1,0:T(8,128)(2,1)S(1)}, bf16[256,128]{1,0:T(8,128)(2,1)S(1)}, u32[]{:S(2)}, u32[]{:S(2)}) collective-permute-start(bf16[256,128]{1,0:T(8,128)(2,1)S(1)} %collective-permute-done.1.refs_3_), channel_id=1, source_target_pairs={{0,1},{1,0},{2,3},{3,2},{4,5},{5,4},{6,7},{7,6},{8,9},{9,8},{10,11... | collective-permute-start | bytes 196616 | tf_op jit(solution)/shard_map/ppermute | solution.py:189
  21.1 3.6 %collective-permute-start.11 = (bf16[4,32,256]{2,1,0:T(8,128)(2,1)S(1)}, bf16[4,32,256]{2,1,0:T(8,128)(2,1)S(1)}, u32[]{:S(2)}, u32[]{:S(2)}) collective-permute-start(bf16[4,32,256]{2,1,0:T(8,128)(2,1)S(1)} %get-tuple-element.30), channel_id=1, source_target_pairs={{0,1},{1,0},{2,3},{3,2},{4,5},{5,4},{6,7},{7,6},{8,9},{9,8},{10,11... | collective-permute-start | bytes 196616 | tf_op jit(solution)/shard_map/ppermute | solution.py:189
  21.1 7.3 %collective-permute-start.10 = (bf16[512,128]{1,0:T(8,128)(2,1)S(1)}, bf16[512,128]{1,0:T(8,128)(2,1)S(1)}, u32[]{:S(2)}, u32[]{:S(2)}) collective-permute-start(bf16[512,128]{1,0:T(8,128)(2,1)S(1)} %get-tuple-element.26.refs_8_), channel_id=1, source_target_pairs={{0,24},{8,16},{16,8},{24,0},{1,25},{9,17},{17,9},{25,1},{2,26},{10... | collective-permute-start | bytes 393224 | tf_op jit(solution)/shard_map/ppermute | solution.py:189
  23.6 7.8 %collective-permute-start.8 = (bf16[512,128]{1,0:T(8,128)(2,1)S(1)}, bf16[512,128]{1,0:T(8,128)(2,1)S(1)}, u32[]{:S(2)}, u32[]{:S(2)}) collective-permute-start(bf16[512,128]{1,0:T(8,128)(2,1)S(1)} %get-tuple-element.26.refs_8_), channel_id=1, source_target_pairs={{0,8},{8,0},{16,24},{24,16},{1,9},{9,1},{17,25},{25,17},{2,10},{10... | collective-permute-start | bytes 393224 | tf_op jit(solution)/shard_map/ppermute | solution.py:189
  24.1 7.2 %collective-permute-start.9 = (bf16[512,128]{1,0:T(8,128)(2,1)S(1)}, bf16[512,128]{1,0:T(8,128)(2,1)S(1)}, u32[]{:S(2)}, u32[]{:S(2)}) collective-permute-start(bf16[512,128]{1,0:T(8,128)(2,1)S(1)} %get-tuple-element.26.refs_8_), channel_id=1, source_target_pairs={{0,16},{8,24},{16,0},{24,8},{1,17},{9,25},{17,1},{25,9},{2,18},{10... | collective-permute-start | bytes 393224 | tf_op jit(solution)/shard_map/ppermute | solution.py:189
  24.7 8.9 %collective-permute-start.12 = (bf16[32,256]{1,0:T(8,128)(2,1)S(1)}, bf16[32,256]{1,0:T(8,128)(2,1)S(1)}, u32[]{:S(2)}, u32[]{:S(2)}) collective-permute-start(bf16[32,256]{1,0:T(8,128)(2,1)S(1)} %get-tuple-element.31), channel_id=1, source_target_pairs={{0,2},{1,3},{2,0},{3,1},{4,6},{5,7},{6,4},{7,5},{8,10},{9,11},{10,... | collective-permute-start | bytes 49160 | tf_op jit(solution)/shard_map/ppermute | solution.py:189
  25.4 8.3 %collective-permute-start.13 = (bf16[32,256]{1,0:T(8,128)(2,1)S(1)}, bf16[32,256]{1,0:T(8,128)(2,1)S(1)}, u32[]{:S(2)}, u32[]{:S(2)}) collective-permute-start(bf16[32,256]{1,0:T(8,128)(2,1)S(1)} %get-tuple-element.33), channel_id=1, source_target_pairs={{0,4},{1,5},{2,6},{3,7},{4,0},{5,1},{6,2},{7,3},{8,12},{9,13},{10,... | collective-permute-start | bytes 49160 | tf_op jit(solution)/shard_map/ppermute | solution.py:189
  28.5 5.5 %collective-permute-start.14 = (bf16[32,256]{1,0:T(8,128)(2,1)S(1)}, bf16[32,256]{1,0:T(8,128)(2,1)S(1)}, u32[]{:S(2)}, u32[]{:S(2)}) collective-permute-start(bf16[32,256]{1,0:T(8,128)(2,1)S(1)} %get-tuple-element.32), channel_id=1, source_target_pairs={{0,6},{1,7},{2,4},{3,5},{4,2},{5,3},{6,0},{7,1},{8,14},{9,15},{10,... | collective-permute-start | bytes 49160 | tf_op jit(solution)/shard_map/ppermute | solution.py:189
